TPU v7x, 32 devices: a whole 2x2x4 slice. The times are simulated.
32 devices in a mesh: grp: 16 (over z, y, core), sub: 2 (over x).
Axes of the slice: x: 2, y: 2, z: 4, core: 2. Of those that a mesh axis runs over, the one named last changes fastest.
Arguments:
- displacement: float32 [128, 32, 256], P('grp', 'sub'), may hold values from -2 to 2
- load: float32 [128, 32, 256], P('grp', 'sub'), may hold values from -6 to 6
- kl_coef: float32 [32], replicated, may hold values from -3 to 3
- damaged: int32 [16], replicated, may hold values from 0 to 1048575, as said below
- owner: int32 [16], replicated, may hold values from 0 to 15, each once
- phase: float32 [16, 32, 1024], P('grp', 'sub'), may hold values from 1 to 10
- soften: float32 [16, 32, 1024], P('grp', 'sub'), may hold values from 0.5 to 4
Outputs:
- step_field: float32 [128, 32, 256], P('grp', 'sub')
- residual: float32 [128, 32, 256], P('grp', 'sub')
- tangents: float32 [16, 9], replicated
- point_flux: float32 [16, 3], replicated
Inputs may be any that keep to these rules, and one draw needn't show every extreme that they name: `damaged`: point p lies in rows p * 8 to (p + 1) * 8 - 1 of the first dimension, so the points are distinct cells. `owner`: each periodic cell resolves exactly one damaged point.
All inputs are finite; a program needn't handle non-finite values.
Results may differ from a plain program's by a relative error of at most 0.00045.
Values sent between devices are 32-bit elements; how exact they have to be, the bound alone decides.
A program may use at most 320 MiB of HBM per device.

v0:
```python
import jax
import jax.numpy as jnp
from jax import lax
from jax.sharding import PartitionSpec as P

M = 32
MITERS = 4
CG_ITERS = 6


K0 = 6.0
SHIFT = 0.002
HIGH = lax.Precision.HIGHEST


def extended(block, sides, width):
    for axis, dim in sides:
        count = lax.axis_size(axis)
        forward = [(i, i + 1) for i in range(count - 1)]
        backward = [(target, source) for source, target in forward]
        low = lax.ppermute(
            lax.slice_in_dim(block, block.shape[dim] - width, None, axis=dim), axis, forward
        )
        high = lax.ppermute(lax.slice_in_dim(block, 0, width, axis=dim), axis, backward)
        block = jnp.concatenate([low, block, high], axis=dim)
    return block


def passed_along(x, axis, by):
    size = lax.axis_size(axis)
    return lax.ppermute(x, axis, [(i, (i + by) % size) for i in range(size)])


def conductivity(kl_coef, xs, ys, zs, total_x, total_y, total_z):
    order = jnp.arange(4, dtype=jnp.float32)[:, None] + 1.0
    base_x = jnp.cos(jnp.pi * order * (xs.astype(jnp.float32)[None] + 0.5) / total_x)
    base_y = jnp.cos(jnp.pi * order * (ys.astype(jnp.float32)[None] + 0.5) / total_y)
    base_z = jnp.cos(jnp.pi * order[:2] * (zs.astype(jnp.float32)[None] + 0.5) / total_z)
    coef = kl_coef.reshape(2, 4, 4)
    field = jnp.einsum("cba,ai,bj,ck->ijk", coef, base_x, base_y, base_z, precision=HIGH)
    return jnp.exp(0.4 * field)


def padded_gradient(field):
    padded = extended(field, (("grp", 0), ("sub", 1)), 1)
    center = padded[:-1, :-1]
    beyond = jnp.concatenate([center[:, :, 1:], jnp.zeros_like(center[:, :, :1])], 2)
    return jnp.stack([padded[1:, :-1] - center, padded[:-1, 1:] - center, beyond - center])


def point_values(grads, flat, in_cells):
    picked = grads.reshape(3, -1)[:, flat]
    local_part = jnp.where(in_cells[None], picked, 0.0).T
    return lax.psum(local_part, ("grp", "sub"))


def divergence(grads, field, kpad, tensors, flat, target):
    flux = kpad[None] * grads
    picked = grads.reshape(3, -1)[:, flat]
    newval = jnp.einsum("pij,jp->ip", tensors, picked, precision=HIGH)
    flux = flux.reshape(3, -1).at[:, target].set(newval, mode="drop").reshape(grads.shape)
    upper_z = flux[2, 1:, 1:]
    lower_z = jnp.pad(upper_z[:, :, :-1], ((0, 0), (0, 0), (1, 0)))
    out = (
        flux[0, :-1, 1:] - flux[0, 1:, 1:] + flux[1, 1:, :-1] - flux[1, 1:, 1:] + lower_z - upper_z
    )
    return out + SHIFT * field


def along_cols(field, table, letter):
    shape = field.shape
    square = field.reshape(shape[:-1] + (M, M))
    if letter == "z":
        result = jnp.einsum("cpyz,zw->cpyw", square, table, precision=HIGH)
    else:
        result = jnp.einsum("cpyz,yw->cpwz", square, table, precision=HIGH)
    return result.reshape(shape)


def along_planes(field, table):
    return jnp.einsum("cxk,xw->cwk", field, table, precision=HIGH)


def tables_for(size):
    freq = jnp.arange(size, dtype=jnp.int32)
    angle = 2.0 * jnp.pi * (freq[:, None] * freq[None, :] % size).astype(jnp.float32) / size
    return (jnp.cos(angle), jnp.sin(angle))


def symbol_block(columns):
    freq = jnp.arange(M, dtype=jnp.int32)
    line = 4.0 * jnp.sin(jnp.pi * freq.astype(jnp.float32) / M) ** 2
    freq_y = columns // M
    freq_z = columns % M
    line_y = 4.0 * jnp.sin(jnp.pi * freq_y.astype(jnp.float32) / M) ** 2
    line_z = 4.0 * jnp.sin(jnp.pi * freq_z.astype(jnp.float32) / M) ** 2
    lam = line[:, None] + (line_y + line_z)[None, :]
    anchor = (freq[:, None] + freq_y[None, :] + freq_z[None, :] == 0).astype(jnp.float32)
    return (1.0 - anchor) / (K0 * float(M * M * M) * (lam + anchor))


def potential_solve(div, inverse, cosine, sine):
    real_part = along_cols(div, cosine, "z")
    imag_part = -along_cols(div, sine, "z")
    real_part, imag_part = (
        along_cols(real_part, cosine, "y") + along_cols(imag_part, sine, "y"),
        along_cols(imag_part, cosine, "y") - along_cols(real_part, sine, "y"),
    )
    joined = lax.all_to_all(
        jnp.stack([real_part, imag_part], 0), "sub", split_axis=3, concat_axis=2, tiled=True
    )
    real_part, imag_part = (joined[0], joined[1])
    real_part, imag_part = (
        along_planes(real_part, cosine) + along_planes(imag_part, sine),
        along_planes(imag_part, cosine) - along_planes(real_part, sine),
    )
    real_part = real_part * inverse[None]
    imag_part = imag_part * inverse[None]
    real_part, imag_part = (
        along_planes(real_part, cosine) - along_planes(imag_part, sine),
        along_planes(real_part, sine) + along_planes(imag_part, cosine),
    )
    joined = lax.all_to_all(
        jnp.stack([real_part, imag_part], 0), "sub", split_axis=2, concat_axis=3, tiled=True
    )
    real_part, imag_part = (joined[0], joined[1])
    real_part, imag_part = (
        along_cols(real_part, cosine, "y") - along_cols(imag_part, sine, "y"),
        along_cols(real_part, sine, "y") + along_cols(imag_part, cosine, "y"),
    )
    return along_cols(real_part, cosine, "z") - along_cols(imag_part, sine, "z")


def cell_strains(phi, units, last_z):
    following = passed_along(phi[:, :1], "sub", -1)
    grad_x = jnp.concatenate([phi[:, 1:], following], 1) - phi
    grad_y = jnp.roll(phi, -M, axis=2) - phi
    next_z = jnp.where(last_z, jnp.roll(phi, M - 1, axis=2), jnp.roll(phi, -1, axis=2))
    grad_z = next_z - phi
    return [units[:, i][:, None, None] + grads for i, grads in enumerate((grad_x, grad_y, grad_z))]


def micro_body(phase, soften, strain):
    planes = phase.shape[1]
    cond = phase[0] / (1.0 + soften[0] * jnp.sum(strain * strain))
    col_block = M * M // lax.axis_size("sub")
    columns = lax.axis_index("sub") * col_block + jnp.arange(col_block, dtype=jnp.int32)
    inverse = symbol_block(columns)
    cosine, sine = tables_for(M)
    units = jnp.eye(3, dtype=jnp.float32)
    col_z = jnp.arange(M * M, dtype=jnp.int32) % M
    last_z = col_z == M - 1
    first_z = col_z == 0
    phi = jnp.zeros((3, planes, M * M), jnp.float32)
    for sweep in range(MITERS):
        parts = cell_strains(phi, units, last_z)
        tau = [(cond - K0) * parts[i] for i in range(3)]
        previous = passed_along(tau[0][:, -1:], "sub", 1)
        div = tau[0] - jnp.concatenate([previous, tau[0][:, :-1]], 1)
        div = div + tau[1] - jnp.roll(tau[1], M, axis=2)
        prior_z = jnp.where(first_z, jnp.roll(tau[2], 1 - M, axis=2), jnp.roll(tau[2], 1, axis=2))
        div = div + tau[2] - prior_z
        phi = potential_solve(div, inverse, cosine, sine)
    parts = cell_strains(phi, units, last_z)
    sums = jnp.stack([jnp.sum(cond[None] * parts[i], axis=(1, 2)) for i in range(3)])
    table = lax.psum(sums, "sub") / float(M * M * M)
    return 0.5 * (table + table.T)


def residual_total(residual):
    return lax.psum(jnp.sum(residual * residual), ("grp", "sub"))


def body(displacement, load, kl_coef, damaged, owner, phase, soften):
    rows_x, rows_y, rows_z = displacement.shape
    grp_index = lax.axis_index("grp")
    sub_index = lax.axis_index("sub")
    total_x = rows_x * lax.axis_size("grp")
    total_y = rows_y * lax.axis_size("sub")
    coord_x = grp_index * rows_x - 1 + jnp.arange(rows_x + 1, dtype=jnp.int32)
    coord_y = sub_index * rows_y - 1 + jnp.arange(rows_y + 1, dtype=jnp.int32)
    coord_z = jnp.arange(rows_z, dtype=jnp.int32)
    inside = ((coord_x >= 0)[:, None, None] & (coord_y >= 0)[None, :, None]).astype(jnp.float32)
    kpad = conductivity(kl_coef, coord_x, coord_y, coord_z, total_x, total_y, rows_z) * inside
    point_z = damaged % rows_z
    rest = damaged // rows_z
    local_x = rest // total_y - grp_index * rows_x + 1
    local_y = rest % total_y - sub_index * rows_y + 1
    in_flux = (local_x >= 0) & (local_x <= rows_x) & (local_y >= 0) & (local_y <= rows_y)
    in_cells = (local_x >= 1) & (local_x <= rows_x) & (local_y >= 1) & (local_y <= rows_y)
    flat = (
        jnp.clip(local_x, 0, rows_x) * (rows_y + 1) + jnp.clip(local_y, 0, rows_y)
    ) * rows_z + point_z
    region = (rows_x + 1) * (rows_y + 1) * rows_z
    target = jnp.where(in_flux, flat, region)
    grads_u = padded_gradient(displacement)
    strains = point_values(grads_u, flat, in_cells)
    select = (owner == grp_index).astype(jnp.float32)
    rve_strain = jnp.sum(select[:, None] * strains, axis=0)
    tangent = micro_body(phase, soften, rve_strain)
    tangents = lax.all_gather(tangent.reshape(1, 9), "grp", axis=0, tiled=True)
    tensors = tangents[owner].reshape(-1, 3, 3)
    rhs = load - divergence(grads_u, displacement, kpad, tensors, flat, target)
    step_field = jnp.zeros_like(rhs)
    residual = rhs
    direction = rhs
    norm_now = residual_total(residual)
    for sweep in range(CG_ITERS):
        image = divergence(padded_gradient(direction), direction, kpad, tensors, flat, target)
        alpha = norm_now / lax.psum(jnp.sum(direction * image), ("grp", "sub"))
        step_field = step_field + alpha * direction
        residual = residual - alpha * image
        norm_next = residual_total(residual)
        direction = residual + norm_next / norm_now * direction
        norm_now = norm_next
    step_grads = point_values(padded_gradient(step_field), flat, in_cells)
    point_flux = jnp.einsum("pij,pj->pi", tensors, step_grads, precision=HIGH)
    return (step_field, residual, tangents, point_flux)


def solution(mesh):
    return jax.shard_map(
        body,
        mesh=mesh,
        in_specs=(
            P("grp", "sub", None),
            P("grp", "sub", None),
            P(),
            P(),
            P(),
            P("grp", "sub", None),
            P("grp", "sub", None),
        ),
        out_specs=(P("grp", "sub", None), P("grp", "sub", None), P(), P()),
        check_vma=False,
    )
```

profile of v0, /device:TPU:0, one launch (start us, length us, event | category | flops | bytes accessed | tf_op | source)
XLA Modules:
  0.0 2054.9 jit_solution(18226921929787480789)
XLA Ops:
  41.8 41.4 %psum.105 = f32[16,3]{1,0:T(8,128)S(1)} all-reduce(f32[16,3]{1,0:T(8,128)S(1)} %fusion.237), channel_id=1, replica_groups=mesh['grp'=16,'sub'=2] {'grp','sub'}, use_global_device_ids=true, to_apply=%region_0.1 | all-reduce | flops 48 | bytes 384 | tf_op jit(solution)/shard_map/psum | solution.py:54
  389.5 11.0 copy.586
  405.7 20.8 %all-gather = f32[16,1,9]{2,1,0:T(1,128)S(1)} all-gather(f32[1,1,9]{2,1,0:T(1,128)S(1)} %reshape.847), channel_id=1, replica_groups=mesh['grp'=16,'sub'=2] {'grp'}, dimensions={0}, use_global_device_ids=true | all-gather | bytes 612 | tf_op jit(solution)/shard_map/all_gather | solution.py:201
  427.5 14.0 scatter_fusion
  441.6 52.6 %fusion.696 = (f32[1,8,16,256]{0,3,2,1:T(8,128)}, f32[1,8,16,256]{0,3,2,1:T(8,128)}, f32[1,8,16,256]{0,3,2,1:T(8,128)}, f32[1,8,16,256]{0,3,2,1:T(8,128)}, f32[1,8,16,256]{0,3,2,1:T(8,128)}) fusion(f32[3,9,17,256]{0,3,2,1:T(8,128)} %bitcast.662), kind=kLoop, calls=%fused_computation.898 | loop fusion | bytes 1310720 | tf_op jit(solution)/shard_map/slice | solution.py:65
  560.1 10.2 copy.592
  577.8 10.2 copy.593
  588.1 14.0 scatter_fusion.1
  602.1 52.8 %fusion.695 = (f32[1,8,16,256]{0,3,2,1:T(8,128)}, f32[1,8,16,256]{0,3,2,1:T(8,128)}, f32[1,8,16,256]{0,3,2,1:T(8,128)}, f32[1,8,16,256]{0,3,2,1:T(8,128)}, f32[1,8,16,256]{0,3,2,1:T(8,128)}) fusion(f32[3,9,17,256]{0,3,2,1:T(8,128)} %bitcast.664), kind=kLoop, calls=%fused_computation.897 | loop fusion | bytes 1310720 | tf_op jit(solution)/shard_map/slice | solution.py:65
  705.3 39.2 %all-reduce.19 = (f32[]{:T(128)}, f32[]{:T(128)}) all-reduce(f32[]{:T(128)} %get-tuple-element.8, f32[]{:T(128)} %get-tuple-element.7), channel_id=1, replica_groups=mesh['grp'=16,'sub'=2] {'grp','sub'}, use_global_device_ids=true, to_apply=%region_9.10 | all-reduce | flops 2 | bytes 16 | tf_op jit(solution)/shard_map/psum | solution.py:171
  746.5 40.9 %psum.109 = f32[]{:T(128)} all-reduce(f32[]{:T(128)} %multiply_reduce_fusion.11), channel_id=1, replica_groups=mesh['grp'=16,'sub'=2] {'grp','sub'}, use_global_device_ids=true, to_apply=%region_14.15 | all-reduce | flops 1 | bytes 8 | tf_op jit(solution)/shard_map/psum | solution.py:171
  804.7 10.2 copy.599
  832.7 14.0 scatter_fusion.2
  846.7 52.8 %fusion.694 = (f32[1,8,16,256]{0,3,2,1:T(8,128)}, f32[1,8,16,256]{0,3,2,1:T(8,128)}, f32[1,8,16,256]{0,3,2,1:T(8,128)}, f32[1,8,16,256]{0,3,2,1:T(8,128)}, f32[1,8,16,256]{0,3,2,1:T(8,128)}) fusion(f32[3,9,17,256]{0,3,2,1:T(8,128)} %bitcast.665), kind=kLoop, calls=%fused_computation.896 | loop fusion | bytes 1310720 | tf_op jit(solution)/shard_map/slice | solution.py:65
  950.0 40.7 %psum.110 = f32[]{:T(128)} all-reduce(f32[]{:T(128)} %get-tuple-element.27), channel_id=1, replica_groups=mesh['grp'=16,'sub'=2] {'grp','sub'}, use_global_device_ids=true, to_apply=%region_17.18 | all-reduce | flops 1 | bytes 8 | tf_op jit(solution)/shard_map/psum | solution.py:210
  992.6 40.1 %psum.111 = f32[]{:T(128)} all-reduce(f32[]{:T(128)} %get-tuple-element.25), channel_id=1, replica_groups=mesh['grp'=16,'sub'=2] {'grp','sub'}, use_global_device_ids=true, to_apply=%region_19.20 | all-reduce | flops 1 | bytes 8 | tf_op jit(solution)/shard_map/psum | solution.py:171
  1079.4 14.0 scatter_fusion.3
  1093.4 52.8 %fusion.693 = (f32[1,8,16,256]{0,3,2,1:T(8,128)}, f32[1,8,16,256]{0,3,2,1:T(8,128)}, f32[1,8,16,256]{0,3,2,1:T(8,128)}, f32[1,8,16,256]{0,3,2,1:T(8,128)}, f32[1,8,16,256]{0,3,2,1:T(8,128)}) fusion(f32[3,9,17,256]{0,3,2,1:T(8,128)} %bitcast.666), kind=kLoop, calls=%fused_computation.895 | loop fusion | bytes 1310720 | tf_op jit(solution)/shard_map/slice | solution.py:65
  1196.7 40.4 %psum.112 = f32[]{:T(128)} all-reduce(f32[]{:T(128)} %get-tuple-element.23), channel_id=1, replica_groups=mesh['grp'=16,'sub'=2] {'grp','sub'}, use_global_device_ids=true, to_apply=%region_22.23 | all-reduce | flops 1 | bytes 8 | tf_op jit(solution)/shard_map/psum | solution.py:210
  1239.1 40.2 %psum.113 = f32[]{:T(128)} all-reduce(f32[]{:T(128)} %get-tuple-element.21), channel_id=1, replica_groups=mesh['grp'=16,'sub'=2] {'grp','sub'}, use_global_device_ids=true, to_apply=%region_24.25 | all-reduce | flops 1 | bytes 8 | tf_op jit(solution)/shard_map/psum | solution.py:171
  1325.2 14.0 scatter_fusion.4
  1339.2 53.1 %fusion.692 = (f32[1,8,16,256]{0,3,2,1:T(8,128)}, f32[1,8,16,256]{0,3,2,1:T(8,128)}, f32[1,8,16,256]{0,3,2,1:T(8,128)}, f32[1,8,16,256]{0,3,2,1:T(8,128)}, f32[1,8,16,256]{0,3,2,1:T(8,128)}) fusion(f32[3,9,17,256]{0,3,2,1:T(8,128)} %bitcast.667), kind=kLoop, calls=%fused_computation.894 | loop fusion | bytes 1310720 | tf_op jit(solution)/shard_map/slice | solution.py:65
  1442.7 40.7 %psum.114 = f32[]{:T(128)} all-reduce(f32[]{:T(128)} %get-tuple-element.19), channel_id=1, replica_groups=mesh['grp'=16,'sub'=2] {'grp','sub'}, use_global_device_ids=true, to_apply=%region_27.28 | all-reduce | flops 1 | bytes 8 | tf_op jit(solution)/shard_map/psum | solution.py:210
  1485.4 39.9 %psum.115 = f32[]{:T(128)} all-reduce(f32[]{:T(128)} %get-tuple-element.17), channel_id=1, replica_groups=mesh['grp'=16,'sub'=2] {'grp','sub'}, use_global_device_ids=true, to_apply=%region_29.30 | all-reduce | flops 1 | bytes 8 | tf_op jit(solution)/shard_map/psum | solution.py:171
  1572.2 14.0 scatter_fusion.5
  1586.2 52.8 %fusion.691 = (f32[1,8,16,256]{0,3,2,1:T(8,128)}, f32[1,8,16,256]{0,3,2,1:T(8,128)}, f32[1,8,16,256]{0,3,2,1:T(8,128)}, f32[1,8,16,256]{0,3,2,1:T(8,128)}, f32[1,8,16,256]{0,3,2,1:T(8,128)}) fusion(f32[3,9,17,256]{0,3,2,1:T(8,128)} %bitcast.668), kind=kLoop, calls=%fused_computation.893 | loop fusion | bytes 1310720 | tf_op jit(solution)/shard_map/slice | solution.py:65
  1689.4 40.4 %psum.116 = f32[]{:T(128)} all-reduce(f32[]{:T(128)} %get-tuple-element.15), channel_id=1, replica_groups=mesh['grp'=16,'sub'=2] {'grp','sub'}, use_global_device_ids=true, to_apply=%region_32.33 | all-reduce | flops 1 | bytes 8 | tf_op jit(solution)/shard_map/psum | solution.py:210
  1731.8 40.2 %psum.117 = f32[]{:T(128)} all-reduce(f32[]{:T(128)} %get-tuple-element.13), channel_id=1, replica_groups=mesh['grp'=16,'sub'=2] {'grp','sub'}, use_global_device_ids=true, to_apply=%region_34.35 | all-reduce | flops 1 | bytes 8 | tf_op jit(solution)/shard_map/psum | solution.py:171
  1818.0 14.0 scatter_fusion.6
  1832.0 52.8 %fusion.690 = (f32[1,8,16,256]{0,3,2,1:T(8,128)}, f32[1,8,16,256]{0,3,2,1:T(8,128)}, f32[1,8,16,256]{0,3,2,1:T(8,128)}, f32[1,8,16,256]{0,3,2,1:T(8,128)}, f32[1,8,16,256]{0,3,2,1:T(8,128)}) fusion(f32[3,9,17,256]{0,3,2,1:T(8,128)} %bitcast.663), kind=kLoop, calls=%fused_computation.892 | loop fusion | bytes 1310720 | tf_op jit(solution)/shard_map/slice | solution.py:65
  1935.3 40.6 %psum.118 = f32[]{:T(128)} all-reduce(f32[]{:T(128)} %get-tuple-element.11), channel_id=1, replica_groups=mesh['grp'=16,'sub'=2] {'grp','sub'}, use_global_device_ids=true, to_apply=%region_37.38 | all-reduce | flops 1 | bytes 8 | tf_op jit(solution)/shard_map/psum | solution.py:210
  2012.1 41.3 %psum.119 = f32[16,3]{1,0:T(8,128)S(1)} all-reduce(f32[16,3]{1,0:T(8,128)S(1)} %broadcast_select_fusion), channel_id=1, replica_groups=mesh['grp'=16,'sub'=2] {'grp','sub'}, use_global_device_ids=true, to_apply=%region_38.39 | all-reduce | flops 48 | bytes 384 | tf_op jit(solution)/shard_map/psum | solution.py:54
  (631 shorter events, 980.0 us)
Async XLA Ops:
  0.7 84.6 %collective-permute-start.4 = (f32[3,1,1024]{2,1,0:T(1,128)S(1)}, f32[3,1,1024]{2,1,0:T(1,128)S(1)}, u32[]{:S(2)}, u32[]{:S(2)}) collective-permute-start(f32[3,1,1024]{2,1,0:T(1,128)S(1)} %slice.710), channel_id=1, source_target_pairs={{0,1},{1,0},{2,3},{3,2},{4,5},{5,4},{6,7},{7,6},{8,9},{9,8},{10,11... | collective-permute-start | bytes 36872 | tf_op jit(solution)/shard_map/ppermute | solution.py:31
  4.4 10.0 collective-permute-start.1
  5.7 7.8 collective-permute-start
  14.5 6.0 collective-permute-start.3
  15.8 5.9 collective-permute-start.2
  86.0 4.0 collective-permute-start.5
  106.3 9.6 all-to-all-start
  153.8 10.8 collective-permute-start.7
  232.9 10.1 collective-permute-start.9
  311.4 9.4 collective-permute-start.11
  340.9 9.3 all-to-all-start.6
  367.3 9.3 all-to-all-start.7
  383.7 3.8 collective-permute-start.12
  549.5 5.3 collective-permute-start.15
  553.4 5.6 collective-permute-start.16
  790.1 5.8 collective-permute-start.18
  798.0 5.6 collective-permute-start.20
  1035.4 5.8 collective-permute-start.22
  1041.2 4.9 collective-permute-start.23
  1044.7 5.6 collective-permute-start.24
  1281.9 5.8 collective-permute-start.26
  1287.7 4.2 collective-permute-start.27
  1290.5 5.6 collective-permute-start.28
  1528.0 5.8 collective-permute-start.30
  1533.8 5.1 collective-permute-start.31
  1537.5 5.6 collective-permute-start.32
  1774.6 5.8 collective-permute-start.34
  1780.4 4.3 collective-permute-start.35
  1783.3 5.6 collective-permute-start.36
  1978.7 5.8 collective-permute-start.38
  1984.5 4.7 collective-permute-start.39
  1987.9 5.6 collective-permute-start.40
  (47 other events, 2935.3 us)
where the time goes:
time: 2070 us; the launch traced here: 2050 us
  local copies, waits for them, and re-layouts  1160 us (56%)
  blocking collectives  595 us (29%)
  waiting for transfers between devices  82.4 us (4%)
  starting transfers between devices  77 us (4%)
  matrix products  59.7 us (3%)
  other arithmetic  57.4 us (3%)
    unnamed x118, local copies, waits for them, and re-layouts  392 us
    slice x7, local copies, waits for them, and re-layouts, divergence(): flux[0, 1:, 1:]  370 us
    psum x6, blocking collectives, residual_total(): return lax.psum(jnp.sum(residual * residual), ('grp', 'sub'))  240 us
    psum x5, blocking collectives, body(): alpha = norm_now / lax.psum(jnp.sum(direction * image), ('grp', 'sub'))  203 us
    scatter x7, local copies, waits for them, and re-layouts, divergence(): flux.reshape(3, -1).at[:, target].set(newval, mode='drop')  98.3 us
    another operation x32, local copies, waits for them, and re-layouts, padded_gradient(): jnp.stack([padded[1:, :-1] - center, padded[:-1, 1:] - center, beyond - c...  85.6 us
    psum x2, blocking collectives, point_values(): return lax.psum(local_part, ('grp', 'sub'))  82.7 us
    mul x8, local copies, waits for them, and re-layouts, divergence(): flux = kpad[None] * grads  72.4 us
  transfers between devices with their start and end apart: 44, of which 28 were waited for; matrix products, arithmetic and copies ran while one was open for 3% of the time, Pallas kernels for 0%

commit v1 on v0

v1 whole, which is shorter than its diff:
```python
import functools
import math

import jax
import jax.numpy as jnp
import numpy as np
from jax import lax
from jax.experimental import pallas as pl
from jax.experimental.pallas import tpu as pltpu
from jax.sharding import PartitionSpec as P

CG_ITERS = 6
STAGES = CG_ITERS + 1
K0 = 6.0
SHIFT = 0.002
MESH = pl.DeviceIdType.MESH
F32 = jnp.float32
BF16 = jnp.bfloat16


def split(x):
    high = x.astype(BF16)
    return high, (x - high.astype(F32)).astype(BF16)


def mm(a, b):
    return jnp.dot(a, b, preferred_element_type=F32)


def total(x):
    while x.ndim > 2:
        x = jnp.sum(x, axis=0)
    return jnp.sum(jnp.sum(x, axis=0, keepdims=True), axis=1, keepdims=True)


def kernel(
    n_grp, n_sub, side, coef, damaged, u_ref, load_ref, owner_ref, phase_ref, soften_ref, table_ref,
    inverse_ref, step_ref, res_ref, tan_ref, grad_ref, field, ys, hx, hy, hc, cells, bc,
    hsend, hrecv, csend, crecv, bsend, brecv, tsend, trecv,
):
    g = lax.axis_index("grp")
    s = lax.axis_index("sub")
    count = n_grp * n_sub
    me = g * n_sub + s
    rows_x, rows_y, rows_z = u_ref.shape
    planes = phase_ref.shape[0]
    total_x, total_y = rows_x * n_grp, rows_y * n_sub

    barrier = pltpu.get_barrier_semaphore()

    def greet(k, carry):
        other = lax.rem(me + k, count)
        pl.semaphore_signal(
            barrier, inc=1, device_id={"grp": other // n_sub, "sub": lax.rem(other, n_sub)},
            device_id_type=MESH,
        )
        return carry

    lax.fori_loop(1, count, greet, 0)
    pl.semaphore_wait(barrier, count - 1)

    g_up, g_down = lax.rem(g + 1, n_grp), lax.rem(g + n_grp - 1, n_grp)
    s_up, s_down = lax.rem(s + 1, n_sub), lax.rem(s + n_sub - 1, n_sub)

    def halo_start(stage, src):
        ys[stage, 0] = src[:, 0:1, :]
        ys[stage, 1] = src[:, rows_y - 1 : rows_y, :]
        moves = (
            (src.at[rows_x - 1], hx.at[stage, 0], g_up, s),
            (src.at[0], hx.at[stage, 1], g_down, s),
            (ys.at[stage, 1], hy.at[stage, 0], g, s_up),
            (ys.at[stage, 0], hy.at[stage, 1], g, s_down),
            (ys.at[stage, 0, rows_x - 1], hc.at[stage, 0], g_up, s_down),
            (ys.at[stage, 1, 0], hc.at[stage, 1], g_down, s_up),
        )
        copies = []
        for i, (a, b, to_g, to_s) in enumerate(moves):
            copy = pltpu.make_async_remote_copy(
                src_ref=a, dst_ref=b, send_sem=hsend.at[stage, i], recv_sem=hrecv.at[stage, i],
                device_id={"grp": to_g, "sub": to_s}, device_id_type=MESH,
            )
            copy.start()
            copies.append(copy)
        return copies

    def halo_wait(stage, copies):
        for copy in copies:
            copy.wait()
        low_x, high_x = (g > 0).astype(F32), (g < n_grp - 1).astype(F32)
        low_y, high_y = (s > 0).astype(F32), (s < n_sub - 1).astype(F32)
        return (
            hx[stage, 0] * low_x, hx[stage, 1] * high_x,
            hy[stage, 0] * low_y, hy[stage, 1] * high_y,
            hc[stage, 0] * (low_x * high_y), hc[stage, 1] * (high_x * low_y),
        )

    def spread_start(stage, row):
        bc[stage, me] = row

        def send(k, carry):
            other = lax.rem(me + k, count)
            pltpu.make_async_remote_copy(
                src_ref=bc.at[stage, me], dst_ref=bc.at[stage, me],
                send_sem=bsend.at[stage], recv_sem=brecv.at[stage],
                device_id={"grp": other // n_sub, "sub": lax.rem(other, n_sub)}, device_id_type=MESH,
            ).start()
            return carry

        lax.fori_loop(1, count, send, 0)

    def spread_wait(stage):
        most = bc.at[stage, pl.ds(0, count - 1)]
        pltpu.make_async_copy(most, most, brecv.at[stage]).wait()
        pltpu.make_async_copy(most, most, bsend.at[stage]).wait()
        return bc[stage]

    own = pl.ds(s * planes, planes)

    def cell_send(k, carry):
        to_s = lax.rem(s + k, n_sub)
        for i, ref in enumerate((phase_ref, soften_ref)):
            pltpu.make_async_remote_copy(
                src_ref=ref, dst_ref=cells.at[i, own], send_sem=csend.at[i], recv_sem=crecv.at[i],
                device_id={"grp": g, "sub": to_s}, device_id_type=MESH,
            ).start()
        return carry

    halo_u = halo_start(0, u_ref)
    lax.fori_loop(1, n_sub, cell_send, 0)
    cells[0, own] = phase_ref[...]
    cells[1, own] = soften_ref[...]

    block = (rows_x, rows_y, rows_z)
    at_x = lax.broadcasted_iota(jnp.int32, block, 0)
    at_y = lax.broadcasted_iota(jnp.int32, block, 1)
    at_z = lax.broadcasted_iota(jnp.int32, block, 2)
    lane = lax.broadcasted_iota(jnp.int32, (1, 128), 1)

    line_z = lax.broadcasted_iota(jnp.int32, (1, rows_z), 1).astype(F32) + 0.5
    cos_z = [jnp.cos(jnp.pi * (c + 1.0) * line_z / rows_z) for c in range(2)]
    pos_y = (s * rows_y + lax.broadcasted_iota(jnp.int32, (rows_y, rows_z), 0)).astype(F32) + 0.5
    low_y = (s * rows_y - 1 + lax.broadcasted_iota(jnp.int32, (1, rows_z), 0)).astype(F32) + 0.5
    pos_x = (g * rows_x + lax.broadcasted_iota(jnp.int32, (rows_x, 1, rows_z), 0)).astype(F32) + 0.5
    low_x = (g * rows_x - 1 + lax.broadcasted_iota(jnp.int32, (1, rows_z), 0)).astype(F32) + 0.5
    cos_y = [jnp.cos(jnp.pi * (b + 1.0) * pos_y / total_y) for b in range(4)]
    cos_yl = [jnp.cos(jnp.pi * (b + 1.0) * low_y / total_y) for b in range(4)]
    log_k = log_x = log_y = 0.0
    for a in range(4):
        rows = [
            coef[a + 4 * b] * cos_z[0] + coef[a + 4 * b + 16] * cos_z[1] for b in range(4)
        ]
        sheet = sum(rows[b] * cos_y[b] for b in range(4))
        strip = sum(rows[b] * cos_yl[b] for b in range(4))
        wave = jnp.cos(jnp.pi * (a + 1.0) * pos_x / total_x)
        log_k = log_k + wave * sheet[None]
        log_y = log_y + wave * strip[None]
        log_x = log_x + jnp.cos(jnp.pi * (a + 1.0) * low_x / total_x) * sheet
    k_own = jnp.exp(0.4 * log_k)
    k_x = jnp.exp(0.4 * log_x) * (g > 0).astype(F32)
    k_y = jnp.exp(0.4 * log_y) * (s > 0).astype(F32)

    def point(p):
        cell = damaged[p]
        rest = cell // rows_z
        return (
            rest // total_y - g * rows_x, lax.rem(rest, total_y) - s * rows_y, lax.rem(cell, rows_z)
        )

    px, py, pz = point(g)
    bx, by, bz = point(lax.max(g - 1, 0))
    hit = (at_x == px) & (at_y == py) & (at_z == pz)
    mask = jnp.where(hit, 1.0, 0.0)
    hit_x = (bx == -1) & (at_y[0] == by) & (at_z[0] == bz)
    mask_x = jnp.where(hit_x, 1.0, 0.0)
    hit_y = (py == -1) & (at_x[:, 0:1] == px) & (at_z[:, 0:1] == pz)
    mask_y = jnp.where(hit_y, 1.0, 0.0)

    def grads_of(v, halos):
        _, high_x, _, high_y, _, _ = halos
        dx = jnp.concatenate([v[1:], high_x[None]], 0) - v
        dy = jnp.where(at_y == rows_y - 1, high_y, pltpu.roll(v, rows_y - 1, 1)) - v
        dz = jnp.where(at_z == rows_z - 1, 0.0, pltpu.roll(v, rows_z - 1, 2)) - v
        return dx, dy, dz

    u = u_ref[...]
    halos_u = halo_wait(0, halo_u)
    grads_u = grads_of(u, halos_u)
    norm = sum(total(d * mask) ** 2 for d in grads_u)
    spread_start(0, jnp.where(lane == g, norm, 0.0))

    for i in range(2):
        most = cells.at[i, pl.ds(0, planes * (n_sub - 1))]
        pltpu.make_async_copy(most, most, crecv.at[i]).wait()
        pltpu.make_async_copy(most, most, csend.at[i]).wait()
    norms = jnp.sum(spread_wait(0), axis=0)
    strength = jnp.sum(jnp.where(owner_ref[...] == g, norms, 0.0), axis=1, keepdims=True)
    cond = cells[0] / (1.0 + cells[1] * strength)
    shift_k = cond - K0
    cube = (side, side, 128)
    cell_lane = lax.broadcasted_iota(jnp.int32, cube, 2)
    group = cell_lane // side
    in_group = lax.rem(cell_lane, side)

    def ahead(v, axis):
        if axis == 0:
            return jnp.concatenate([v[1:], v[:1]], 0)
        if axis == 1:
            return pltpu.roll(v, side - 1, 1)
        return jnp.where(in_group == side - 1, pltpu.roll(v, side - 1, 2), pltpu.roll(v, 127, 2))

    def behind(v, axis):
        if axis == 0:
            return jnp.concatenate([v[-1:], v[:-1]], 0)
        if axis == 1:
            return pltpu.roll(v, 1, 1)
        return jnp.where(in_group == 0, pltpu.roll(v, 129 - side, 2), pltpu.roll(v, 1, 2))

    wide = side * 8
    tz = table_ref[4, 0:128, 0:128], table_ref[5, 0:128, 0:128]
    ty = table_ref[0], table_ref[1]
    tx = table_ref[2], table_ref[3]

    def right(v):
        high, low = split(v.reshape(side * side, 128))
        return (mm(high, tz[0]) + mm(low, tz[0]) + mm(high, tz[1])).reshape(cube)

    def left(t, v):
        high, low = split(v)
        return mm(t[0], high) + mm(t[0], low) + mm(t[1], high)

    def along_y(v):
        flat = v.reshape(side * side, 128)
        parts = [left(ty, flat[i : i + wide]) for i in range(0, side * side, wide)]
        return jnp.concatenate(parts, 0).reshape(cube)

    def along_x(v):
        parts = [
            left(tx, v[:, i : i + 8].reshape(wide, 128)).reshape(side, 8, 128)
            for i in range(0, side, 8)
        ]
        return jnp.concatenate(parts, 1)

    def solve(div):
        spectrum = along_x(along_y(right(div))) * inverse_ref[...]
        return right(along_y(along_x(spectrum)))

    def div_of(phi):
        out = 0.0
        for axis in range(3):
            tau = shift_k * (ahead(phi, axis) - phi)
            out = out + tau - behind(tau, axis)
        return out

    back = jnp.where(group == 0, behind(shift_k, 0), shift_k)
    back = jnp.where(group == 1, behind(shift_k, 1), back)
    back = jnp.where(group == 2, behind(shift_k, 2), back)
    div1 = shift_k - back
    phi1 = solve(div1)
    div2 = div_of(phi1)
    phi2 = solve(div2)
    div3 = div_of(phi2)
    first, second = div1 + div2, div2 + div3
    points = float(side**3)
    mean = total(cond) / (points * (128 // side))
    entry = {}
    for turn in range(3):
        a = phi1 if turn == 0 else pltpu.roll(phi1, turn * side, 2)
        b = phi2 if turn == 0 else pltpu.roll(phi2, turn * side, 2)
        sums = jnp.sum(jnp.sum(a * first + b * second, axis=0), axis=0, keepdims=True)
        for j in range(turn, 3):
            value = -jnp.sum(
                jnp.where(lane // side == j, sums, 0.0), axis=1, keepdims=True
            ) / points
            entry[j - turn, j] = entry[j, j - turn] = value + mean if turn == 0 else value
    row = jnp.zeros((1, 128), F32)
    for i in range(3):
        for j in range(3):
            row = row + jnp.where(lane == 3 * i + j, entry[i, j], 0.0)
    tan_ref[g] = row

    def tangent_send(k, carry):
        pltpu.make_async_remote_copy(
            src_ref=tan_ref.at[g], dst_ref=tan_ref.at[g], send_sem=tsend, recv_sem=trecv,
            device_id={"grp": lax.rem(g + k, n_grp), "sub": s}, device_id_type=MESH,
        ).start()
        return carry

    lax.fori_loop(1, n_grp, tangent_send, 0)
    most = tan_ref.at[pl.ds(0, n_grp - 1)]
    pltpu.make_async_copy(most, most, trecv).wait()
    pltpu.make_async_copy(most, most, tsend).wait()
    tangents = tan_ref[...]
    which = lax.broadcasted_iota(jnp.int32, (n_grp, 1, 128), 0)

    def tensor(p):
        who = jnp.sum(jnp.where(lane == p, owner_ref[...], 0).astype(F32), axis=1, keepdims=True)
        mine = jnp.sum(jnp.where(which.astype(F32) == who, tangents, 0.0), axis=0)
        return {
            (i, j): jnp.sum(jnp.where(lane == 3 * i + j, mine, 0.0), axis=1, keepdims=True)
            for i in range(3) for j in range(i, 3)
        }

    t_own, t_before = tensor(g), tensor(lax.max(g - 1, 0))
    k00, k11, k22 = (k_own + mask * (t_own[i, i] - k_own) for i in range(3))
    k01, k02, k12 = (mask * t_own[i] for i in ((0, 1), (0, 2), (1, 2)))
    x00 = k_x + mask_x * (t_before[0, 0] - k_x)
    x01, x02 = mask_x * t_before[0, 1], mask_x * t_before[0, 2]
    y11 = k_y + mask_y * (t_own[1, 1] - k_y)
    y01, y12 = mask_y * t_own[0, 1], mask_y * t_own[1, 2]

    def operate(v, halos, grads):
        low_x, _, low_y, _, corner_x, corner_y = halos
        dx, dy, dz = grads
        q0 = k00 * dx + k01 * dy + k02 * dz
        q1 = k01 * dx + k11 * dy + k12 * dz
        q2 = k02 * dx + k12 * dy + k22 * dz
        edge_y, edge_z = at_y[0] == rows_y - 1, at_z[0] == rows_z - 1
        below_x = (
            x00 * (v[0] - low_x)
            + x01 * (jnp.where(edge_y, corner_x, pltpu.roll(low_x, rows_y - 1, 0)) - low_x)
            + x02 * (jnp.where(edge_z, 0.0, pltpu.roll(low_x, rows_z - 1, 1)) - low_x)
        )
        below_y = (
            y11 * (v[:, 0:1] - low_y)
            + y01 * (jnp.concatenate([low_y[1:], corner_y[None]], 0) - low_y)
            + y12
            * (jnp.where(at_z[:, 0:1] == rows_z - 1, 0.0, pltpu.roll(low_y, rows_z - 1, 2)) - low_y)
        )
        out = jnp.concatenate([below_x[None], q0[:-1]], 0) - q0
        out = out + jnp.where(at_y == 0, below_y, pltpu.roll(q1, 1, 1)) - q1
        out = out + jnp.where(at_z == 0, 0.0, pltpu.roll(q2, 1, 2)) - q2
        return out + SHIFT * v

    def picks(grads):
        return [total(d * mask) for d in grads]

    def row_of(values):
        out = jnp.zeros((1, 128), F32)
        for i, value in enumerate(values):
            out = out + jnp.where(lane == i, value, 0.0)
        return out

    r = load_ref[...] - operate(u, halos_u, grads_u)
    field[0] = r
    copies = halo_start(1, field.at[0])
    halos = halo_wait(1, copies)
    grads = grads_of(r, halos)
    w = operate(r, halos, grads)
    at_points = picks(grads)
    alpha = beta = gamma = None
    for step in range(CG_ITERS):
        last = step == CG_ITERS - 1
        if not last:
            field[step + 1] = w
            copies = halo_start(step + 2, field.at[step + 1])
        spread_start(step + 1, row_of([total(r * r), total(r * w)] + at_points))
        if not last:
            halos = halo_wait(step + 2, copies)
            grads = grads_of(w, halos)
            n = operate(w, halos, grads)
            at_points = picks(grads)
        got = spread_wait(step + 1)
        sums = jnp.sum(got, axis=0)
        new = sums[:, 0:1]
        delta = sums[:, 1:2]
        if step == 0:
            alpha = new / delta
            point_r = got
            point_p = point_r
            point_x = alpha * point_p
            p, sv = r, w
            x = alpha * p
        else:
            beta = new / gamma
            point_s = got if step == 1 else got + beta_before * point_s
            point_r = point_r - alpha * point_s
            alpha_new = new / (delta - beta * new / alpha)
            point_p = point_r + beta * point_p
            point_x = point_x + alpha_new * point_p
            alpha = alpha_new
            p = r + beta * p
            sv = w + beta * sv
            x = x + alpha * p
        r = r - alpha * sv
        if not last:
            z = n if step == 0 else n + beta * z
            w = w - alpha * z
        gamma, beta_before = new, beta
    step_ref[...] = x
    res_ref[...] = r
    grad_ref[...] = point_x


def tables(side):
    index = np.arange(side)
    angle = 2.0 * np.pi * (np.outer(index, index) % side) / side
    hartley = (np.cos(angle) + np.sin(angle)) / np.sqrt(side)
    wide = side * 8
    kinds = np.zeros((3, wide, wide), np.float64)
    kinds[0] = np.kron(np.eye(8), hartley)
    kinds[1] = np.kron(hartley, np.eye(8))
    kinds[2, :128, :128] = np.kron(np.eye(128 // side), hartley)
    kinds = kinds.astype(np.float32)
    high = kinds.astype(jnp.bfloat16)
    low = (kinds - high.astype(np.float32)).astype(jnp.bfloat16)
    table = np.stack([high, low], 1).reshape(6, wide, wide)
    line = 4.0 * np.sin(np.pi * index / side) ** 2
    lam = line[:, None, None] + line[None, :, None] + line[None, None, :]
    lam[0, 0, 0] = 1.0
    inverse = 1.0 / (K0 * lam)
    inverse[0, 0, 0] = 0.0
    return table, np.tile(inverse.astype(np.float32), (1, 1, 128 // side))


def body(displacement, load, kl_coef, damaged, owner, phase, soften):
    n_grp, n_sub = lax.axis_size("grp"), lax.axis_size("sub")
    count = n_grp * n_sub
    rows_x, rows_y, rows_z = displacement.shape
    planes = phase.shape[1]
    side = math.isqrt(phase.shape[2])
    table, inverse = tables(side)
    lanes = [
        jnp.tile(a.reshape(planes, side, side), (1, 1, 128 // side)) for a in (phase, soften)
    ]
    points = owner.shape[0]
    owners = jnp.pad(owner, (0, 128 - points), constant_values=-1).reshape(1, 128)
    vmem = pl.BlockSpec(memory_space=pltpu.VMEM)
    smem = pl.BlockSpec(memory_space=pltpu.SMEM)
    step_field, residual, rows, slopes = pl.pallas_call(
        functools.partial(kernel, n_grp, n_sub, side),
        out_shape=[
            jax.ShapeDtypeStruct(displacement.shape, F32),
            jax.ShapeDtypeStruct(displacement.shape, F32),
            jax.ShapeDtypeStruct((n_grp, 1, 128), F32),
            jax.ShapeDtypeStruct((count, 1, 128), F32),
        ],
        in_specs=[smem, smem] + [vmem] * 7,
        out_specs=[vmem] * 4,
        scratch_shapes=[
            pltpu.VMEM((CG_ITERS, rows_x, rows_y, rows_z), F32),
            pltpu.VMEM((STAGES, 2, rows_x, 1, rows_z), F32),
            pltpu.VMEM((STAGES, 2, rows_y, rows_z), F32),
            pltpu.VMEM((STAGES, 2, rows_x, 1, rows_z), F32),
            pltpu.VMEM((STAGES, 2, 1, rows_z), F32),
            pltpu.VMEM((2, side, side, 128), F32),
            pltpu.VMEM((STAGES, count, 1, 128), F32),
            pltpu.SemaphoreType.DMA((STAGES, 6)),
            pltpu.SemaphoreType.DMA((STAGES, 6)),
            pltpu.SemaphoreType.DMA((2,)),
            pltpu.SemaphoreType.DMA((2,)),
            pltpu.SemaphoreType.DMA((STAGES,)),
            pltpu.SemaphoreType.DMA((STAGES,)),
            pltpu.SemaphoreType.DMA,
            pltpu.SemaphoreType.DMA,
        ],
        compiler_params=pltpu.CompilerParams(collective_id=0, has_side_effects=True),
    )(kl_coef, damaged, displacement, load, owners, *lanes, jnp.asarray(table), jnp.asarray(inverse))
    tangents = rows[:, 0, :9]
    slopes = jnp.sum(slopes.reshape(points, -1, 128), axis=1)[:, 2:5]
    tensors = tangents[owner].reshape(-1, 3, 3)
    point_flux = jnp.sum(tensors * slopes[:, None, :], axis=2)
    return step_field, residual, tangents, point_flux


def solution(mesh):
    return jax.shard_map(
        body,
        mesh=mesh,
        in_specs=(
            P("grp", "sub", None), P("grp", "sub", None), P(), P(), P(),
            P("grp", "sub", None), P("grp", "sub", None),
        ),
        out_specs=(P("grp", "sub", None), P("grp", "sub", None), P(), P()),
        check_vma=False,
    )
```

time: 2070 us -> 81.2 us (0.04)
  local copies, waits for them, and re-layouts: 1160 us -> 7.96 us
  blocking collectives: 595 us -> 0 us
  waiting for transfers between devices: 82.4 us -> 0 us
  starting transfers between devices: 77 us -> 0 us
  Pallas kernels: 0 us -> 70.9 us
  matrix products: 59.7 us -> 0 us
  other arithmetic: 57.4 us -> 1.35 us
    psum x14 -> x0, blocking collectives: 531 us -> none  [the longest x6 240 us: residual_total(): return lax.psum(jnp.sum(residual * residual), ('grp', 'sub'))]
    unnamed x118 -> x13, local copies, waits for them, and re-layouts: 392 us -> 2.87 us
    slice x83 -> x2, local copies, waits for them, and re-layouts: 380 us -> 0.16 us  [body(): slopes = jnp.sum(slopes.reshape(points, -1, 128), axis=1)[:, 2:5]]
    another operation x48 -> x6, local copies, waits for them, and re-layouts: 106 us -> 3.76 us  [body(): jnp.tile(a.reshape(planes, side, side), (1, 1, 128 // side))]
    scatter x7 -> x0, local copies, waits for them, and re-layouts: 98.3 us -> none  [divergence(): flux.reshape(3, -1).at[:, target].set(newval, mode='drop')]
    mul x10 -> x0, local copies, waits for them, and re-layouts: 73.5 us -> none  [the longest x8 72.4 us: divergence(): flux = kpad[None] * grads]
    pallas_call x0 -> x1, Pallas kernels: none -> 70.9 us  [body(): pl.pallas_call(functools.partial(kernel, n_grp, n_sub, side), out_shape=[...]
    ppermute x41 -> x0, starting transfers between devices: 66.4 us -> none  [the longest x16 39.3 us: extended(): lax.ppermute(lax.slice_in_dim(block, block.shape[dim] - width, None, axis...]
  transfers between devices with their start and end apart: 44 -> 0, of which waited for: 28 -> 0; matrix products, arithmetic and copies ran while one was open for 3% -> 0% of each run, Pallas kernels for 0% -> 0%
where the time goes in v1:
time: 81.2 us; the launch traced here: 80.9 us
  Pallas kernels  70.9 us (87%)
  local copies, waits for them, and re-layouts  7.96 us (10%)
  other arithmetic  1.35 us (2%)
    pallas_call x1, Pallas kernels, body(): pl.pallas_call(functools.partial(kernel, n_grp, n_sub, side), out_shape=[...  70.9 us
    another operation x6, local copies, waits for them, and re-layouts, body(): jnp.tile(a.reshape(planes, side, side), (1, 1, 128 // side))  3.76 us
    unnamed x13, local copies, waits for them, and re-layouts  2.87 us

profile of v1, /device:TPU:0, one launch (start us, length us, event | category | flops | bytes accessed | tf_op | source)
XLA Modules:
  0.0 80.9 jit_solution(3731765853204288920)
XLA Ops:
  0.6 1.0 %tile.20 = f32[16,32,32]{2,1,0:T(8,128)S(1)} reshape(f32[1,16,1024]{2,1,0:T(8,128)} %param.14) | data formatting | bytes 131072 | tf_op jit(solution)/shard_map/tile | solution.py:423
  1.6 0.2 tile.21
  1.8 0.0 copy-start.3
  1.8 1.2 %tile.22.phase_ref = f32[16,32,128]{2,1,0:T(8,128)} reshape(f32[16,32,4,32]{3,2,1,0:T(4,128)S(1)} %tile.21) | data formatting | bytes 524288 | tf_op jit(solution)/shard_map/tile | solution.py:423
  3.0 0.0 copy-done.3
  3.0 0.1 tile.23
  3.1 0.2 tile.24
  3.3 0.0 copy-start.4
  3.3 1.2 %tile.25.soften_ref = f32[16,32,128]{2,1,0:T(8,128)} reshape(f32[16,32,4,32]{3,2,1,0:T(4,128)S(1)} %tile.24) | data formatting | bytes 524288 | tf_op jit(solution)/shard_map/tile | solution.py:423
  4.4 0.0 copy-done.4
  4.4 0.5 pad_bitcast_fusion.owner_ref
  5.0 70.9 %shard_map.120 = (f32[8,16,256]{2,1,0:T(8,128)}, f32[8,16,256]{2,1,0:T(8,128)}, f32[16,1,128]{2,1,0:T(1,128)}, f32[32,1,128]{2,1,0:T(1,128)}) custom-call(f32[32]{0:T(128)} %coef.1, s32[16]{0:T(128)} %damaged.1, f32[8,16,256]{2,1,0:T(8,128)} %u_ref.1, f32[8,16,256]{2,1,0:T(8,128)} %load_ref.1, s32[1,128]{1,0:T(1,128)} %pad_bitcast_fusion.owner_ref, ...), custom_call_target="tpu_custom_call" | custom-call | tf_op jit(solution)/shard_map/pallas_call | solution.py:429
  75.9 0.0 copy-start
  75.9 0.0 copy-start.2
  75.9 0.7 copy-done
  76.6 0.6 gather_fusion
  77.1 0.1 copy.14
  77.2 0.7 reduce_sum.18
  78.0 0.1 slice.10
  78.0 0.1 copy.15
  78.1 0.6 multiply_reduce_fusion
  78.7 0.0 copy-done.2
  78.7 0.0 copy-start.1
  78.7 0.7 copy.19
  79.4 0.3 copy-done.1
  79.7 0.7 copy.20
  80.3 0.6 copy.21
  (3 shorter events, 0.0 us)
Async XLA Ops:
  1.8 1.2 %copy-start.3 = (f32[1,16,1024]{2,1,0:T(8,128)S(1)}, f32[1,16,1024]{2,1,0:T(8,128)}, u32[]{:S(2)}) copy-start(f32[1,16,1024]{2,1,0:T(8,128)} %param.15) | copy-start | bytes 196612
  3.3 1.2 %copy-start.4 = (s32[16]{0:T(128)S(1)}, s32[16]{0:T(128)}, u32[]{:S(2)}) copy-start(s32[16]{0:T(128)} %param.13) | copy-start | bytes 196
  75.9 0.7 copy-start
  75.9 2.9 %copy-start.2 = (f32[8,16,256]{2,1,0:T(8,128)S(1)}, f32[8,16,256]{2,1,0:T(8,128)}, u32[]{:S(2)}) copy-start(f32[8,16,256]{2,1,0:T(8,128)} %get-tuple-element.16) | copy-start | bytes 393220
  78.7 1.0 %copy-start.1 = (f32[8,16,256]{2,1,0:T(8,128)S(1)}, f32[8,16,256]{2,1,0:T(8,128)}, u32[]{:S(2)}) copy-start(f32[8,16,256]{2,1,0:T(8,128)} %get-tuple-element.17) | copy-start | bytes 393220

commit v2 on v1

--- a/solution.py
+++ b/solution.py
@@ -34,18 +34,24 @@
 
 
 def kernel(
-    n_grp, n_sub, side, coef, damaged, u_ref, load_ref, owner_ref, phase_ref, soften_ref, table_ref,
-    inverse_ref, step_ref, res_ref, tan_ref, grad_ref, field, ys, hx, hy, hc, cells, bc,
-    hsend, hrecv, csend, crecv, bsend, brecv, tsend, trecv,
+    n_grp, n_sub, side, coef, damaged, owners, u_ref, load_ref, owner_ref, cell_ref, table_any,
+    inverse_any, step_ref, res_ref, tan_ref, flux_ref, field, ys, hx, hy, hc, cells, bc, chosen,
+    table_ref, inverse_ref, hsend, hrecv, csend, crecv, bsend, brecv, tsend, trecv, fetch,
 ):
     g = lax.axis_index("grp")
     s = lax.axis_index("sub")
     count = n_grp * n_sub
     me = g * n_sub + s
     rows_x, rows_y, rows_z = u_ref.shape
-    planes = phase_ref.shape[0]
+    planes = cell_ref.shape[0]
     total_x, total_y = rows_x * n_grp, rows_y * n_sub
 
+    fetches = [
+        pltpu.make_async_copy(a, b, fetch.at[i])
+        for i, (a, b) in enumerate(((table_any, table_ref), (inverse_any, inverse_ref)))
+    ]
+    for copy in fetches:
+        copy.start()
     barrier = pltpu.get_barrier_semaphore()
 
     def greet(k, carry):
@@ -57,79 +63,6 @@
         return carry
 
     lax.fori_loop(1, count, greet, 0)
-    pl.semaphore_wait(barrier, count - 1)
-
-    g_up, g_down = lax.rem(g + 1, n_grp), lax.rem(g + n_grp - 1, n_grp)
-    s_up, s_down = lax.rem(s + 1, n_sub), lax.rem(s + n_sub - 1, n_sub)
-
-    def halo_start(stage, src):
-        ys[stage, 0] = src[:, 0:1, :]
-        ys[stage, 1] = src[:, rows_y - 1 : rows_y, :]
-        moves = (
-            (src.at[rows_x - 1], hx.at[stage, 0], g_up, s),
-            (src.at[0], hx.at[stage, 1], g_down, s),
-            (ys.at[stage, 1], hy.at[stage, 0], g, s_up),
-            (ys.at[stage, 0], hy.at[stage, 1], g, s_down),
-            (ys.at[stage, 0, rows_x - 1], hc.at[stage, 0], g_up, s_down),
-            (ys.at[stage, 1, 0], hc.at[stage, 1], g_down, s_up),
-        )
-        copies = []
-        for i, (a, b, to_g, to_s) in enumerate(moves):
-            copy = pltpu.make_async_remote_copy(
-                src_ref=a, dst_ref=b, send_sem=hsend.at[stage, i], recv_sem=hrecv.at[stage, i],
-                device_id={"grp": to_g, "sub": to_s}, device_id_type=MESH,
-            )
-            copy.start()
-            copies.append(copy)
-        return copies
-
-    def halo_wait(stage, copies):
-        for copy in copies:
-            copy.wait()
-        low_x, high_x = (g > 0).astype(F32), (g < n_grp - 1).astype(F32)
-        low_y, high_y = (s > 0).astype(F32), (s < n_sub - 1).astype(F32)
-        return (
-            hx[stage, 0] * low_x, hx[stage, 1] * high_x,
-            hy[stage, 0] * low_y, hy[stage, 1] * high_y,
-            hc[stage, 0] * (low_x * high_y), hc[stage, 1] * (high_x * low_y),
-        )
-
-    def spread_start(stage, row):
-        bc[stage, me] = row
-
-        def send(k, carry):
-            other = lax.rem(me + k, count)
-            pltpu.make_async_remote_copy(
-                src_ref=bc.at[stage, me], dst_ref=bc.at[stage, me],
-                send_sem=bsend.at[stage], recv_sem=brecv.at[stage],
-                device_id={"grp": other // n_sub, "sub": lax.rem(other, n_sub)}, device_id_type=MESH,
-            ).start()
-            return carry
-
-        lax.fori_loop(1, count, send, 0)
-
-    def spread_wait(stage):
-        most = bc.at[stage, pl.ds(0, count - 1)]
-        pltpu.make_async_copy(most, most, brecv.at[stage]).wait()
-        pltpu.make_async_copy(most, most, bsend.at[stage]).wait()
-        return bc[stage]
-
-    own = pl.ds(s * planes, planes)
-
-    def cell_send(k, carry):
-        to_s = lax.rem(s + k, n_sub)
-        for i, ref in enumerate((phase_ref, soften_ref)):
-            pltpu.make_async_remote_copy(
-                src_ref=ref, dst_ref=cells.at[i, own], send_sem=csend.at[i], recv_sem=crecv.at[i],
-                device_id={"grp": g, "sub": to_s}, device_id_type=MESH,
-            ).start()
-        return carry
-
-    halo_u = halo_start(0, u_ref)
-    lax.fori_loop(1, n_sub, cell_send, 0)
-    cells[0, own] = phase_ref[...]
-    cells[1, own] = soften_ref[...]
-
     block = (rows_x, rows_y, rows_z)
     at_x = lax.broadcasted_iota(jnp.int32, block, 0)
     at_y = lax.broadcasted_iota(jnp.int32, block, 1)
@@ -175,6 +108,77 @@
     hit_y = (py == -1) & (at_x[:, 0:1] == px) & (at_z[:, 0:1] == pz)
     mask_y = jnp.where(hit_y, 1.0, 0.0)
 
+    pl.semaphore_wait(barrier, count - 1)
+
+    g_up, g_down = lax.rem(g + 1, n_grp), lax.rem(g + n_grp - 1, n_grp)
+    s_up, s_down = lax.rem(s + 1, n_sub), lax.rem(s + n_sub - 1, n_sub)
+
+    def halo_start(stage, src):
+        ys[stage, 0] = src[:, 0:1, :]
+        ys[stage, 1] = src[:, rows_y - 1 : rows_y, :]
+        moves = (
+            (src.at[rows_x - 1], hx.at[stage, 0], g_up, s),
+            (src.at[0], hx.at[stage, 1], g_down, s),
+            (ys.at[stage, 1], hy.at[stage, 0], g, s_up),
+            (ys.at[stage, 0], hy.at[stage, 1], g, s_down),
+            (ys.at[stage, 0, rows_x - 1], hc.at[stage, 0], g_up, s_down),
+            (ys.at[stage, 1, 0], hc.at[stage, 1], g_down, s_up),
+        )
+        copies = []
+        for i, (a, b, to_g, to_s) in enumerate(moves):
+            copy = pltpu.make_async_remote_copy(
+                src_ref=a, dst_ref=b, send_sem=hsend.at[stage, i], recv_sem=hrecv.at[stage, i],
+                device_id={"grp": to_g, "sub": to_s}, device_id_type=MESH,
+            )
+            copy.start()
+            copies.append(copy)
+        return copies
+
+    def halo_wait(stage, copies):
+        for copy in copies:
+            copy.wait()
+        low_x, high_x = (g > 0).astype(F32), (g < n_grp - 1).astype(F32)
+        low_y, high_y = (s > 0).astype(F32), (s < n_sub - 1).astype(F32)
+        return (
+            hx[stage, 0] * low_x, hx[stage, 1] * high_x,
+            hy[stage, 0] * low_y, hy[stage, 1] * high_y,
+            hc[stage, 0] * (low_x * high_y), hc[stage, 1] * (high_x * low_y),
+        )
+
+    def spread_start(stage, row):
+        bc[stage, me] = row
+
+        def send(k, carry):
+            other = lax.rem(me + k, count)
+            pltpu.make_async_remote_copy(
+                src_ref=bc.at[stage, me], dst_ref=bc.at[stage, me],
+                send_sem=bsend.at[stage], recv_sem=brecv.at[stage],
+                device_id={"grp": other // n_sub, "sub": lax.rem(other, n_sub)}, device_id_type=MESH,
+            ).start()
+            return carry
+
+        lax.fori_loop(1, count, send, 0)
+
+    def spread_wait(stage):
+        most = bc.at[stage, pl.ds(0, count - 1)]
+        pltpu.make_async_copy(most, most, brecv.at[stage]).wait()
+        pltpu.make_async_copy(most, most, bsend.at[stage]).wait()
+        return bc[stage]
+
+    own = pl.ds(s * planes, planes)
+
+    def cell_send(k, carry):
+        to_s = lax.rem(s + k, n_sub)
+        pltpu.make_async_remote_copy(
+            src_ref=cell_ref, dst_ref=cells.at[own], send_sem=csend, recv_sem=crecv,
+            device_id={"grp": g, "sub": to_s}, device_id_type=MESH,
+        ).start()
+        return carry
+
+    halo_u = halo_start(0, u_ref)
+    lax.fori_loop(1, n_sub, cell_send, 0)
+    cells[own] = cell_ref[...]
+
     def grads_of(v, halos):
         _, high_x, _, high_y, _, _ = halos
         dx = jnp.concatenate([v[1:], high_x[None]], 0) - v
@@ -188,13 +192,32 @@
     norm = sum(total(d * mask) ** 2 for d in grads_u)
     spread_start(0, jnp.where(lane == g, norm, 0.0))
 
-    for i in range(2):
-        most = cells.at[i, pl.ds(0, planes * (n_sub - 1))]
-        pltpu.make_async_copy(most, most, crecv.at[i]).wait()
-        pltpu.make_async_copy(most, most, csend.at[i]).wait()
+    most = cells.at[pl.ds(0, planes * (n_sub - 1))]
+    pltpu.make_async_copy(most, most, crecv).wait()
+    pltpu.make_async_copy(most, most, csend).wait()
+    for copy in fetches:
+        copy.wait()
+    packed = cells[...]
+    turned = [packed] + [pltpu.roll(packed, i * side, 2) for i in range(1, 4)]
+    set_of = lax.broadcasted_iota(jnp.int32, packed.shape, 2) // side
+
+    def unpack(at):
+        out = turned[(0 - at) % 4]
+        for j in range(1, 4):
+            out = jnp.where(set_of == j, turned[(j - at) % 4], out)
+        return out
+
+    def planes_of(low, high):
+        parts = []
+        for i in range(n_sub):
+            parts += [unpack(low)[i * planes : (i + 1) * planes]]
+            parts += [unpack(high)[i * planes : (i + 1) * planes]]
+        return jnp.concatenate(parts, 0)
+
+    cell_phase, cell_soften = planes_of(0, 2), planes_of(1, 3)
     norms = jnp.sum(spread_wait(0), axis=0)
     strength = jnp.sum(jnp.where(owner_ref[...] == g, norms, 0.0), axis=1, keepdims=True)
-    cond = cells[0] / (1.0 + cells[1] * strength)
+    cond = cell_phase / (1.0 + cell_soften * strength)
     shift_k = cond - K0
     cube = (side, side, 128)
     cell_lane = lax.broadcasted_iota(jnp.int32, cube, 2)
@@ -340,55 +363,111 @@
             out = out + jnp.where(lane == i, value, 0.0)
         return out
 
-    r = load_ref[...] - operate(u, halos_u, grads_u)
-    field[0] = r
-    copies = halo_start(1, field.at[0])
-    halos = halo_wait(1, copies)
-    grads = grads_of(r, halos)
-    w = operate(r, halos, grads)
-    at_points = picks(grads)
-    alpha = beta = gamma = None
-    for step in range(CG_ITERS):
-        last = step == CG_ITERS - 1
-        if not last:
-            field[step + 1] = w
-            copies = halo_start(step + 2, field.at[step + 1])
-        spread_start(step + 1, row_of([total(r * r), total(r * w)] + at_points))
-        if not last:
-            halos = halo_wait(step + 2, copies)
-            grads = grads_of(w, halos)
-            n = operate(w, halos, grads)
-            at_points = picks(grads)
+    def apply(stage, v, meanwhile=None):
+        field[stage - 1] = v
+        copies = halo_start(stage, field.at[stage - 1])
+        if meanwhile is not None:
+            meanwhile()
+        halos = halo_wait(stage, copies)
+        grads = grads_of(v, halos)
+        return operate(v, halos, grads), picks(grads)
+
+    def choose():
+        for q in range(flux_ref.shape[0]):
+            chosen[q] = jnp.sum(jnp.where(which == owners[q], tangents, 0.0), axis=0)
+
+    r = [load_ref[...] - operate(u, halos_u, grads_u)]
+    v, slope0 = apply(1, r[0], choose)
+    r.append(v)
+    v, slope1 = apply(2, r[1])
+    r.append(v)
+    x = point_x = 0.0
+    p = gp = None
+    gamma = alpha = r3_before = g2_before = None
+
+    def steps(r, p, scalars, depth):
+        (first, one), (second, two) = scalars
+        p = r if p is None else [a + first * b for a, b in zip(r, p)]
+        move = one * p[0]
+        r = [r[j] - one * p[j + 1] for j in range(depth)]
+        middle = r[-1]
+        p = [a + second * b for a, b in zip(r, p)]
+        move = move + two * p[0]
+        r = [r[j] - two * p[j + 1] for j in range(depth - 1)]
+        return r, p, move, middle
+
+    blocks = CG_ITERS // 2
+    for step in range(blocks):
+        last = step == blocks - 1
+
+        def send(step=step, r=r, p=p, slopes=slope0 + slope1):
+            dots = [total(r[0] * r[0]), total(r[0] * r[1]), total(r[1] * r[1]), total(r[1] * r[2])]
+            if p is not None:
+                dots += [total(r[1] * p[1]), total(p[1] * p[1])]
+                dots += [total(p[1] * r[2]), total(p[1] * p[2])]
+            else:
+                dots += [jnp.zeros((1, 1), F32)] * 4
+            spread_start(step + 1, row_of(dots + slopes))
+
+        if last:
+            send()
+        else:
+            r3, slope0 = apply(3 + 2 * step, r[2], send)
+            r4, slope1 = apply(4 + 2 * step, r3)
         got = spread_wait(step + 1)
         sums = jnp.sum(got, axis=0)
-        new = sums[:, 0:1]
-        delta = sums[:, 1:2]
+        m00, m01, m11, m12, c11, d11, c12, d12 = (sums[:, i : i + 1] for i in range(8))
         if step == 0:
-            alpha = new / delta
-            point_r = got
-            point_p = point_r
-            point_x = alpha * point_p
-            p, sv = r, w
-            x = alpha * p
+            first, one = jnp.zeros((1, 1), F32), m00 / m01
         else:
-            beta = new / gamma
-            point_s = got if step == 1 else got + beta_before * point_s
-            point_r = point_r - alpha * point_s
-            alpha_new = new / (delta - beta * new / alpha)
-            point_p = point_r + beta * point_p
-            point_x = point_x + alpha_new * point_p
-            alpha = alpha_new
-            p = r + beta * p
-            sv = w + beta * sv
-            x = x + alpha * p
-        r = r - alpha * sv
-        if not last:
-            z = n if step == 0 else n + beta * z
-            w = w - alpha * z
-        gamma, beta_before = new, beta
+            first = m00 / gamma
+            one = m00 / (m01 - first * m00 / alpha)
+        image_square = m11 + first * (2.0 * c11 + first * d11)
+        cross = m11 + first * c11
+        image_energy = m12 + first * (2.0 * c12 + first * d12)
+        m00_next = one * one * image_square - m00
+        m01_next = m01 - 2.0 * one * cross + one * one * image_energy
+        second = m00_next / m00
+        two = m00_next / (m01_next - second * m00_next / one)
+        scalars = (first, one), (second, two)
+
+        fresh = [got, pltpu.roll(got, 125, 2)]
+        if step == 0:
+            gr = fresh
+        else:
+            if gp is not None:
+                gp = gp + [(g2_before - fresh[0]) / alpha_before]
+            gr, gp, move, g2_before = steps(gr + fresh, gp, scalars_before, 3)
+            point_x = point_x + move
+        if last:
+            (first, one), (second, two) = scalars
+            q0 = gr[0] + first * gp[0]
+            q1 = gr[1] + first * gp[1]
+            point_x = point_x + one * q0 + two * (gr[0] - one * q1 + second * q0)
+
+        if last:
+            r, p, move, _ = steps(r, p, scalars, 2)
+        else:
+            if p is not None:
+                p = p + [(r3_before - r3) / alpha]
+            r, p, move, r3_before = steps(r + [r3, r4], p, scalars, 4)
+        x = x + move
+        scalars_before, alpha_before = scalars, alpha
+        gamma, alpha = m00_next, two
     step_ref[...] = x
-    res_ref[...] = r
-    grad_ref[...] = point_x
+    res_ref[...] = r[0]
+    points = flux_ref.shape[0]
+    slope = jnp.sum(point_x.reshape(points, n_sub, 1, 128), axis=1)
+    spot = lax.broadcasted_iota(jnp.int32, slope.shape, 2)
+    product = 0.0
+    for j in range(3):
+        part = jnp.sum(jnp.where(spot == 8 + j, slope, 0.0), axis=2, keepdims=True)
+        product = product + jnp.where((lax.rem(spot, 3) == j) & (spot < 9), chosen[...], 0.0) * part
+    out = jnp.zeros_like(slope)
+    for i in range(3):
+        part = jnp.sum(jnp.where(spot // 3 == i, product, 0.0), axis=2, keepdims=True)
+        out = out + jnp.where(spot == i, part, 0.0)
+    flux_ref[...] = out
 
 
 def tables(side):
@@ -419,22 +498,22 @@
     planes = phase.shape[1]
     side = math.isqrt(phase.shape[2])
     table, inverse = tables(side)
-    lanes = [
-        jnp.tile(a.reshape(planes, side, side), (1, 1, 128 // side)) for a in (phase, soften)
-    ]
+    half = planes // 2
+    cubes = [a.reshape(planes, side, side) for a in (phase, soften)]
+    packed = jnp.concatenate([a[i : i + half] for i in (0, half) for a in cubes], axis=2)
     points = owner.shape[0]
     owners = jnp.pad(owner, (0, 128 - points), constant_values=-1).reshape(1, 128)
     vmem = pl.BlockSpec(memory_space=pltpu.VMEM)
     smem = pl.BlockSpec(memory_space=pltpu.SMEM)
-    step_field, residual, rows, slopes = pl.pallas_call(
+    step_field, residual, rows, flux = pl.pallas_call(
         functools.partial(kernel, n_grp, n_sub, side),
         out_shape=[
             jax.ShapeDtypeStruct(displacement.shape, F32),
             jax.ShapeDtypeStruct(displacement.shape, F32),
             jax.ShapeDtypeStruct((n_grp, 1, 128), F32),
-            jax.ShapeDtypeStruct((count, 1, 128), F32),
+            jax.ShapeDtypeStruct((points, 1, 128), F32),
         ],
-        in_specs=[smem, smem] + [vmem] * 7,
+        in_specs=[smem] * 3 + [vmem] * 4 + [pl.BlockSpec(memory_space=pl.ANY)] * 2,
         out_specs=[vmem] * 4,
         scratch_shapes=[
             pltpu.VMEM((CG_ITERS, rows_x, rows_y, rows_z), F32),
@@ -442,24 +521,24 @@
             pltpu.VMEM((STAGES, 2, rows_y, rows_z), F32),
             pltpu.VMEM((STAGES, 2, rows_x, 1, rows_z), F32),
             pltpu.VMEM((STAGES, 2, 1, rows_z), F32),
-            pltpu.VMEM((2, side, side, 128), F32),
-            pltpu.VMEM((STAGES, count, 1, 128), F32),
+            pltpu.VMEM((half * n_sub, side, 128), F32),
+            pltpu.VMEM((CG_ITERS // 2 + 1, count, 1, 128), F32),
+            pltpu.VMEM((points, 1, 128), F32),
+            pltpu.VMEM(table.shape, BF16),
+            pltpu.VMEM(inverse.shape, F32),
             pltpu.SemaphoreType.DMA((STAGES, 6)),
             pltpu.SemaphoreType.DMA((STAGES, 6)),
-            pltpu.SemaphoreType.DMA((2,)),
-            pltpu.SemaphoreType.DMA((2,)),
+            pltpu.SemaphoreType.DMA,
+            pltpu.SemaphoreType.DMA,
             pltpu.SemaphoreType.DMA((STAGES,)),
             pltpu.SemaphoreType.DMA((STAGES,)),
             pltpu.SemaphoreType.DMA,
             pltpu.SemaphoreType.DMA,
+            pltpu.SemaphoreType.DMA((2,)),
         ],
         compiler_params=pltpu.CompilerParams(collective_id=0, has_side_effects=True),
-    )(kl_coef, damaged, displacement, load, owners, *lanes, jnp.asarray(table), jnp.asarray(inverse))
-    tangents = rows[:, 0, :9]
-    slopes = jnp.sum(slopes.reshape(points, -1, 128), axis=1)[:, 2:5]
-    tensors = tangents[owner].reshape(-1, 3, 3)
-    point_flux = jnp.sum(tensors * slopes[:, None, :], axis=2)
-    return step_field, residual, tangents, point_flux
+    )(kl_coef, damaged, owner, displacement, load, owners, packed, jnp.asarray(table), jnp.asarray(inverse))
+    return step_field, residual, rows[:, 0, :9], flux[:, 0, :3]
 
 
 def solution(mesh):

time: 81.2 us -> 70 us (0.86)
  Pallas kernels: 70.9 us -> 61.5 us
  local copies, waits for them, and re-layouts: 7.96 us -> 6.66 us
    pallas_call x1, Pallas kernels: 70.9 us -> 61.5 us  [body(): pl.pallas_call(functools.partial(kernel, n_grp, n_sub, side), out_shape=[...]
    another operation x6 -> x0, local copies, waits for them, and re-layouts: 3.76 us -> none  [body(): jnp.tile(a.reshape(planes, side, side), (1, 1, 128 // side))]
    slice x2 -> x7, local copies, waits for them, and re-layouts: 0.16 us -> 1.81 us  [the longest x6 1.15 us: body(): a[i:i + half]]
    unnamed x13, local copies, waits for them, and re-layouts: 2.87 us -> 4.34 us
    reduce_sum x2 -> x0, other arithmetic: 1.34 us -> none  [the longest x1 0.74 us: body(): slopes = jnp.sum(slopes.reshape(points, -1, 128), axis=1)[:, 2:5]]
    concatenate x0 -> x1, other arithmetic: none -> 0.83 us  [body(): jnp.concatenate([a[i:i + half] for i in (0, half) for a in cubes], axis=2)]
where the time goes in v2:
time: 70 us; the launch traced here: 69.6 us
  Pallas kernels  61.5 us (88%)
  local copies, waits for them, and re-layouts  6.66 us (10%)
  other arithmetic  0.83 us (1%)
    pallas_call x1, Pallas kernels, body(): pl.pallas_call(functools.partial(kernel, n_grp, n_sub, side), out_shape=[...  61.5 us
    unnamed x13, local copies, waits for them, and re-layouts  4.34 us

profile of v2, /device:TPU:0, one launch (start us, length us, event | category | flops | bytes accessed | tf_op | source)
XLA Modules:
  0.0 69.6 jit_solution(3371261702494925161)
XLA Ops:
  0.6 0.8 %fusion = (f32[1,8,1024]{2,1,0:T(8,128)S(1)}, f32[1,8,1024]{2,1,0:T(8,128)S(1)}) fusion(f32[1,16,1024]{2,1,0:T(8,128)} %param.14), kind=kLoop, calls=%fused_computation.2 | loop fusion | bytes 131072 | tf_op jit(solution)/shard_map/slice | solution.py:503
  1.4 0.0 copy-start.1
  1.4 0.1 slice.31
  1.5 0.7 %copy-done.1 = f32[1,16,1024]{2,1,0:T(8,128)S(1)} copy-done((f32[1,16,1024]{2,1,0:T(8,128)S(1)}, f32[1,16,1024]{2,1,0:T(8,128)}, u32[]{:S(2)}) %copy-start.1) | copy-done | bytes 65560
  2.3 0.1 slice.33
  2.4 0.1 slice.35
  2.4 0.1 slice.37
  2.5 0.0 copy-start.4
  2.5 0.8 %pad_maximum_fusion.cell_ref = f32[8,32,128]{2,1,0:T(8,128)} fusion(f32[8,32,32]{2,1,0:T(8,128)S(1)} %slice.37, f32[8,32,32]{2,1,0:T(8,128)S(1)} %slice.35, f32[8,32,32]{2,1,0:T(8,128)S(1)} %slice.33, f32[8,32,32]{2,1,0:T(8,128)S(1)} %slice.31), kind=kLoop, calls=%fused_computation | loop fusion | flops 98304 | bytes 262144 | tf_op jit(solution)/shard_map/concatenate | solution.py:503
  3.4 0.0 copy-done.4
  3.4 0.5 pad_bitcast_fusion.owner_ref
  3.9 61.5 %shard_map.120 = (f32[8,16,256]{2,1,0:T(8,128)}, f32[8,16,256]{2,1,0:T(8,128)}, f32[16,1,128]{2,1,0:T(1,128)}, f32[16,1,128]{2,1,0:T(1,128)}) custom-call(f32[32]{0:T(128)} %coef.1, s32[16]{0:T(128)} %damaged.1, s32[16]{0:T(128)} %owners.1, f32[8,16,256]{2,1,0:T(8,128)} %u_ref.1, f32[8,16,256]{2,1,0:T(8,128)} %load_ref.1, ...), custom_call_target="tpu_custom_call" | custom-call | tf_op jit(solution)/shard_map/pallas_call | solution.py:508
  65.4 0.0 copy-start.2
  65.4 0.7 copy-done.2
  66.1 0.7 copy.13
  66.7 0.0 copy-start
  66.7 1.6 %copy.17 = f32[8,16,256]{2,1,0:T(8,128)} copy(f32[8,16,256]{2,1,0:T(8,128)} %get-tuple-element.20) | data formatting | bytes 262144
  68.3 0.0 copy-done
  68.3 0.0 copy-start.3
  68.3 0.7 copy.18
  69.0 0.0 copy-done.3
  69.0 0.6 copy.19
  (1 shorter events, 0.0 us)
Async XLA Ops:
  1.4 0.8 %copy-start.1 = (f32[1,16,1024]{2,1,0:T(8,128)S(1)}, f32[1,16,1024]{2,1,0:T(8,128)}, u32[]{:S(2)}) copy-start(f32[1,16,1024]{2,1,0:T(8,128)} %param.15) | copy-start | bytes 196612
  2.5 0.8 %copy-start.4 = (s32[16]{0:T(128)S(1)}, s32[16]{0:T(128)}, u32[]{:S(2)}) copy-start(s32[16]{0:T(128)} %owners.1) | copy-start | bytes 196
  65.4 0.7 %copy-start.2 = (f32[16,1,128]{2,1,0:T(1,128)S(1)}, f32[16,1,128]{2,1,0:T(1,128)}, u32[]{:S(2)}) copy-start(f32[16,1,128]{2,1,0:T(1,128)} %get-tuple-element.11) | copy-start | bytes 24580
  66.7 1.6 %copy-start = (f32[8,16,256]{2,1,0:T(8,128)S(1)}, f32[8,16,256]{2,1,0:T(8,128)}, u32[]{:S(2)}) copy-start(f32[8,16,256]{2,1,0:T(8,128)} %get-tuple-element.21) | copy-start | bytes 393220
  68.3 0.7 %copy-start.3 = (f32[16,1,128]{2,1,0:T(1,128)S(1)}, f32[16,1,128]{2,1,0:T(1,128)}, u32[]{:S(2)}) copy-start(f32[16,1,128]{2,1,0:T(1,128)} %get-tuple-element.10) | copy-start | bytes 24580
